TPU v7x, 256 devices: a whole 4x4x8 slice. The times are simulated.
256 devices in a mesh: dom: 64 (over z, y, core), chan: 4 (over x).
Axes of the slice: x: 4, y: 4, z: 8, core: 2. Of those that a mesh axis runs over, the one named last changes fastest.
Arguments:
- features: bfloat16 [256, 65536], P('chan', 'dom'), may hold values from -6 to 6
- cotangent: bfloat16 [256, 65536], P('chan', 'dom'), may hold values from -6 to 6
- weights: bfloat16 [9, 256, 256], P(None, 'chan'), may hold values from -0.375 to 0.375
- tile_values: float32 [4096, 128, 128], P('dom'), may hold values from -0.046875 to 0.046875
- tile_cols: int32 [64, 8, 8], P('dom'), may hold values from 0 to 11, as said below
- send_list: int32 [64, 4, 128], P('dom'), may hold values from 0 to 1023
Outputs:
- input_grad: float32 [256, 65536], P('chan', 'dom')
- weight_grad: float32 [9, 256, 256], P(None, None, 'chan')
Inputs may be any that keep to these rules, and one draw needn't show every extreme that they name: `tile_cols`: values below 8 are blocks of the partition's own nodes; 8 + s is the block received from neighbour slot s. Tile 0 of row block r has column block r.
All inputs are finite; a program needn't handle non-finite values.
Results may differ from a plain program's by a relative error of at most 0.0003.
Values may be sent and summed in bfloat16 or wider, within the bound.
A program may use at most 128 MiB of HBM per device.

v0:
```python
import jax
import jax.numpy as jnp
from jax import lax
from jax.sharding import PartitionSpec as P

NEIGHBOUR_SHIFTS = (1, -1, 2, -2)


def from_behind(block, axis, distance):
    devices = range(lax.axis_size(axis))
    route = [((i - distance) % len(devices), i) for i in devices]
    return lax.ppermute(block, axis, route)


def exchange_rows(outgoing):
    received = [
        from_behind(outgoing[:, slot_index], "dom", offset)
        for slot_index, offset in enumerate(NEIGHBOUR_SHIFTS)
    ]
    return received


def apply_operator(field_in, tile_values, tile_cols, send_list):
    channels, local_nodes = field_in.shape
    tile_size = tile_values.shape[-1]
    per_row = tile_cols.shape[-1]
    outgoing = jnp.take(field_in, send_list[0], axis=1)
    received = exchange_rows(outgoing)
    extended = jnp.concatenate([field_in] + received, axis=1)
    blocks = extended.reshape(channels, -1, tile_size)
    picked = jnp.take(blocks, tile_cols.reshape(-1), axis=1)
    product = jnp.einsum("ctj,tjk->ctk", picked, tile_values, precision=lax.Precision.HIGHEST)
    return (
        product.reshape(channels, -1, per_row, tile_size).sum(axis=2).reshape(channels, local_nodes)
    )


def local(features, cotangent, weights, tile_values, tile_cols, send_list):
    top_order = weights.shape[0] - 1
    local_nodes = features.shape[1]

    def operator_on(field_in):
        return apply_operator(field_in, tile_values, tile_cols, send_list)

    feat_all, cot_all = (
        lax.all_gather(features, "chan", axis=0, tiled=True),
        lax.all_gather(cotangent, "chan", axis=0, tiled=True),
    )
    feat_wide = feat_all.astype(jnp.float32)

    def mixed_term(order_index):
        return jnp.dot(weights[order_index], cot_all, preferred_element_type=jnp.float32)

    def grad_term(state):
        return lax.dot_general(
            feat_wide, state, (((1,), (1,)), ((), ())), precision=lax.Precision.HIGHEST
        )

    cheb_prev = cotangent.astype(jnp.float32)
    grad_terms = [grad_term(cheb_prev)]
    cheb_now = operator_on(cheb_prev)
    grad_terms.append(grad_term(cheb_now))
    for order_index in range(2, top_order + 1):
        cheb_prev, cheb_now = (cheb_now, 2.0 * operator_on(cheb_now) - cheb_prev)
        grad_terms.append(grad_term(cheb_now))
    current = mixed_term(top_order)
    clen_later = jnp.zeros_like(current)
    for order_index in range(top_order - 1, 0, -1):
        current, clen_later = (
            mixed_term(order_index) + 2.0 * operator_on(current) - clen_later,
            current,
        )
    input_grad = mixed_term(0) + operator_on(current) - clen_later
    local_grads = jnp.stack(grad_terms)
    summed = lax.psum(local_grads, "dom")
    nodes_all = lax.axis_size("dom") * local_nodes
    return (input_grad, summed * float(nodes_all) ** (-0.5))


def solution(mesh):
    placed = (
        P("chan", "dom"),
        P("chan", "dom"),
        P(None, "chan", None),
        P("dom", None, None),
        P("dom", None, None),
        P("dom", None, None),
    )
    return jax.shard_map(
        local,
        mesh=mesh,
        in_specs=placed,
        out_specs=(P("chan", "dom"), P(None, None, "chan")),
        check_vma=False,
    )
```

profile of v0, /device:TPU:2, one launch (start us, length us, event | category | flops | bytes accessed | tf_op | source)
XLA Modules:
  0.0 664.3 jit_solution(9862079954037837758)
XLA Ops:
  8.6 13.7 %all_gather.6 = bf16[256,1024]{1,0:T(8,128)(2,1)S(1)} all-gather(bf16[64,1024]{1,0:T(8,128)(2,1)} %param.11), channel_id=1, replica_groups=mesh['dom'=64,'chan'=4] {'chan'}, dimensions={0}, use_global_device_ids=true | all-gather | bytes 655360 | tf_op jit(solution)/shard_map/all_gather | solution.py:47
  38.1 12.8 %all_gather.7 = bf16[256,1024]{1,0:T(8,128)(2,1)S(1)} all-gather(bf16[64,1024]{1,0:T(8,128)(2,1)S(1)} %copy-done.13), channel_id=1, replica_groups=mesh['dom'=64,'chan'=4] {'chan'}, dimensions={0}, use_global_device_ids=true | all-gather | bytes 655360 | tf_op jit(solution)/shard_map/all_gather | solution.py:46
  57.3 7.7 %collective-permute-done.34 = f32[64,128]{0,1:T(8,128)S(1)} collective-permute-done((f32[64,128]{0,1:T(8,128)S(1)}, f32[64,128]{0,1:T(8,128)S(1)}, u32[]{:S(2)}, u32[]{:S(2)}) %collective-permute-start.34) | collective-permute-done | bytes 32800 | tf_op jit(solution)/shard_map/ppermute | solution.py:12
  70.4 6.4 bitcast_reduce_fusion.7
  88.4 6.7 %bitcast_reduce_fusion.15 = f32[64,8,128]{2,0,1:T(8,128)S(1)} fusion(f32[64,128,128]{2,1,0:T(8,128)} %param.13, f32[64,64,128]{2,1,0:T(8,128)} %gather_fusion.1, pred[64]{0:T(512)(128)(4,1)S(1)} %compare_and_fusion), kind=kOutput, calls=%fused_computation.47 | convolution fusion | flops 806289408 | bytes 6553664 | tf_op jit(solution)/shard_map/ctj,tjk->ctk/dot_general | solution.py:32
  123.1 6.7 %bitcast_reduce_fusion.14 = f32[64,8,128]{2,0,1:T(8,128)S(1)} fusion(f32[64,128,128]{2,1,0:T(8,128)} %param.13, f32[64,64,128]{2,1,0:T(8,128)} %gather_fusion.3, pred[64]{0:T(512)(128)(4,1)S(1)} %compare_and_fusion), kind=kOutput, calls=%fused_computation.46 | convolution fusion | flops 806289408 | bytes 6553664 | tf_op jit(solution)/shard_map/ctj,tjk->ctk/dot_general | solution.py:32
  152.7 6.7 %bitcast_reduce_fusion.6 = f32[64,8,128]{2,0,1:T(8,128)S(1)} fusion(f32[64,128,128]{2,1,0:T(8,128)} %param.13, f32[64,64,128]{2,1,0:T(8,128)} %gather_fusion.19, pred[64]{0:T(512)(128)(4,1)S(1)} %compare_and_fusion), kind=kOutput, calls=%fused_computation.38 | convolution fusion | flops 806289408 | bytes 6553664 | tf_op jit(solution)/shard_map/ctj,tjk->ctk/dot_general | solution.py:32
  179.7 6.7 %bitcast_reduce_fusion.13 = f32[64,8,128]{2,0,1:T(8,128)S(1)} fusion(f32[64,128,128]{2,1,0:T(8,128)} %param.13, f32[64,64,128]{2,1,0:T(8,128)} %gather_fusion.5, pred[64]{0:T(512)(128)(4,1)S(1)} %compare_and_fusion), kind=kOutput, calls=%fused_computation.45 | convolution fusion | flops 806289408 | bytes 6553664 | tf_op jit(solution)/shard_map/ctj,tjk->ctk/dot_general | solution.py:32
  198.1 5.6 collective-permute-start.15
  210.0 6.7 %bitcast_reduce_fusion.5 = f32[64,8,128]{2,0,1:T(8,128)S(1)} fusion(f32[64,128,128]{2,1,0:T(8,128)} %param.13, f32[64,64,128]{2,1,0:T(8,128)} %gather_fusion.21, pred[64]{0:T(512)(128)(4,1)S(1)} %compare_and_fusion), kind=kOutput, calls=%fused_computation.37 | convolution fusion | flops 806289408 | bytes 6553664 | tf_op jit(solution)/shard_map/ctj,tjk->ctk/dot_general | solution.py:32
  230.5 5.8 collective-permute-start.47
  242.1 6.7 %bitcast_reduce_fusion.12 = f32[64,8,128]{2,0,1:T(8,128)S(1)} fusion(f32[64,128,128]{2,1,0:T(8,128)} %param.13, f32[64,64,128]{2,1,0:T(8,128)} %gather_fusion.7, pred[64]{0:T(512)(128)(4,1)S(1)} %compare_and_fusion), kind=kOutput, calls=%fused_computation.44 | convolution fusion | flops 806289408 | bytes 6553664 | tf_op jit(solution)/shard_map/ctj,tjk->ctk/dot_general | solution.py:32
  270.7 6.7 %bitcast_reduce_fusion.4 = f32[64,8,128]{2,0,1:T(8,128)S(1)} fusion(f32[64,128,128]{2,1,0:T(8,128)} %param.13, f32[64,64,128]{2,1,0:T(8,128)} %gather_fusion.23, pred[64]{0:T(512)(128)(4,1)S(1)} %compare_and_fusion), kind=kOutput, calls=%fused_computation.36 | convolution fusion | flops 806289408 | bytes 6553664 | tf_op jit(solution)/shard_map/ctj,tjk->ctk/dot_general | solution.py:32
  297.4 6.7 %bitcast_reduce_fusion.11 = f32[64,8,128]{2,0,1:T(8,128)S(1)} fusion(f32[64,128,128]{2,1,0:T(8,128)} %param.13, f32[64,64,128]{2,1,0:T(8,128)} %gather_fusion.9, pred[64]{0:T(512)(128)(4,1)S(1)} %compare_and_fusion), kind=kOutput, calls=%fused_computation.43 | convolution fusion | flops 806289408 | bytes 6553664 | tf_op jit(solution)/shard_map/ctj,tjk->ctk/dot_general | solution.py:32
  325.5 6.7 %bitcast_reduce_fusion.3 = f32[64,8,128]{2,0,1:T(8,128)S(1)} fusion(f32[64,128,128]{2,1,0:T(8,128)} %param.13, f32[64,64,128]{2,1,0:T(8,128)} %gather_fusion.25, pred[64]{0:T(512)(128)(4,1)S(1)} %compare_and_fusion), kind=kOutput, calls=%fused_computation.35 | convolution fusion | flops 806289408 | bytes 6553664 | tf_op jit(solution)/shard_map/ctj,tjk->ctk/dot_general | solution.py:32
  341.6 5.8 collective-permute-start.55
  349.5 6.7 %bitcast_reduce_fusion.10 = f32[64,8,128]{2,0,1:T(8,128)S(1)} fusion(f32[64,128,128]{2,1,0:T(8,128)} %param.13, f32[64,64,128]{2,1,0:T(8,128)} %gather_fusion.11, pred[64]{0:T(512)(128)(4,1)S(1)} %compare_and_fusion), kind=kOutput, calls=%fused_computation.42 | convolution fusion | flops 806289408 | bytes 6553664 | tf_op jit(solution)/shard_map/ctj,tjk->ctk/dot_general | solution.py:32
  378.1 6.7 %bitcast_reduce_fusion.2 = f32[64,8,128]{2,0,1:T(8,128)S(1)} fusion(f32[64,128,128]{2,1,0:T(8,128)} %param.13, f32[64,64,128]{2,1,0:T(8,128)} %gather_fusion.27, pred[64]{0:T(512)(128)(4,1)S(1)} %compare_and_fusion), kind=kOutput, calls=%fused_computation.34 | convolution fusion | flops 806289408 | bytes 6553664 | tf_op jit(solution)/shard_map/ctj,tjk->ctk/dot_general | solution.py:32
  404.7 6.7 %bitcast_reduce_fusion.9 = f32[64,8,128]{2,0,1:T(8,128)S(1)} fusion(f32[64,128,128]{2,1,0:T(8,128)} %param.13, f32[64,64,128]{2,1,0:T(8,128)} %gather_fusion.13, pred[64]{0:T(512)(128)(4,1)S(1)} %compare_and_fusion), kind=kOutput, calls=%fused_computation.41 | convolution fusion | flops 806289408 | bytes 6553664 | tf_op jit(solution)/shard_map/ctj,tjk->ctk/dot_general | solution.py:32
  433.5 6.7 %bitcast_reduce_fusion.1 = f32[64,8,128]{2,0,1:T(8,128)S(1)} fusion(f32[64,128,128]{2,1,0:T(8,128)} %param.13, f32[64,64,128]{2,1,0:T(8,128)} %gather_fusion.29, pred[64]{0:T(512)(128)(4,1)S(1)} %compare_and_fusion), kind=kOutput, calls=%fused_computation.33 | convolution fusion | flops 806289408 | bytes 6553664 | tf_op jit(solution)/shard_map/ctj,tjk->ctk/dot_general | solution.py:32
  450.4 5.6 collective-permute-start.63
  465.5 6.7 %bitcast_reduce_fusion = f32[64,8,128]{2,0,1:T(8,128)S(1)} fusion(f32[64,128,128]{2,1,0:T(8,128)} %param.13, f32[64,64,128]{2,1,0:T(8,128)} %gather_fusion.31, pred[64]{0:T(512)(128)(4,1)S(1)} %compare_and_fusion), kind=kOutput, calls=%fused_computation.32 | convolution fusion | flops 806289408 | bytes 6553664 | tf_op jit(solution)/shard_map/ctj,tjk->ctk/dot_general | solution.py:32
  473.8 6.7 %bitcast_reduce_fusion.8 = f32[64,8,128]{2,0,1:T(8,128)S(1)} fusion(f32[64,128,128]{2,1,0:T(8,128)} %param.13, f32[64,64,128]{2,1,0:T(8,128)} %gather_fusion.15, pred[64]{0:T(512)(128)(4,1)S(1)} %compare_and_fusion), kind=kOutput, calls=%fused_computation.40 | convolution fusion | flops 806289408 | bytes 6553664 | tf_op jit(solution)/shard_map/ctj,tjk->ctk/dot_general | solution.py:32
  482.2 172.9 %all-reduce.2.cloned.1.call-done = f32[9,256,64]{1,2,0:T(8,128)} async-done(((f32[9,256,64]{1,2,0:T(8,128)}), f32[9,256,64]{1,2,0:T(8,128)}) %all-reduce.2.cloned.1.call-update) | async-done | bytes 589840 | tf_op jit(solution)/shard_map/psum | solution.py:75
  (368 shorter events, 312.0 us)
Async XLA Ops:
  7.2 647.9 %all-reduce.2.cloned.1.call-start = ((), (), s32[]{:S(2)}) async-start(), calls=%async_computation | async-start | bytes 1179648 | tf_op jit(solution)/shard_map/psum | solution.py:75
  26.1 52.7 %collective-permute-start = (f32[64,128]{1,0:T(8,128)}, f32[64,128]{1,0:T(8,128)}, u32[]{:S(2)}, u32[]{:S(2)}) collective-permute-start(f32[64,128]{1,0:T(8,128)} %get-tuple-element.67), channel_id=1, source_target_pairs={{252,0},{0,4},{4,8},{8,12},{12,16},{16,20},{20,24},{24,28},{28,32}... | collective-permute-start | bytes 98312 | tf_op jit(solution)/shard_map/ppermute | solution.py:12
  26.1 54.0 %collective-permute-start.1 = (f32[64,128]{1,0:T(8,128)}, f32[64,128]{1,0:T(8,128)}, u32[]{:S(2)}, u32[]{:S(2)}) collective-permute-start(f32[64,128]{1,0:T(8,128)} %get-tuple-element.66), channel_id=1, source_target_pairs={{4,0},{8,4},{12,8},{16,12},{20,16},{24,20},{28,24},{32,28},{36,32}... | collective-permute-start | bytes 98312 | tf_op jit(solution)/shard_map/ppermute | solution.py:12
  31.2 50.4 %collective-permute-start.2 = (f32[64,128]{1,0:T(8,128)}, f32[64,128]{1,0:T(8,128)}, u32[]{:S(2)}, u32[]{:S(2)}) collective-permute-start(f32[64,128]{1,0:T(8,128)} %get-tuple-element.65), channel_id=1, source_target_pairs={{248,0},{252,4},{0,8},{4,12},{8,16},{12,20},{16,24},{20,28},{24,32... | collective-permute-start | bytes 98312 | tf_op jit(solution)/shard_map/ppermute | solution.py:12
  31.2 52.8 %collective-permute-start.3 = (f32[64,128]{1,0:T(8,128)}, f32[64,128]{1,0:T(8,128)}, u32[]{:S(2)}, u32[]{:S(2)}) collective-permute-start(f32[64,128]{1,0:T(8,128)} %get-tuple-element.64), channel_id=1, source_target_pairs={{8,0},{12,4},{16,8},{20,12},{24,16},{28,20},{32,24},{36,28},{40,32... | collective-permute-start | bytes 98312 | tf_op jit(solution)/shard_map/ppermute | solution.py:12
  132.8 34.2 %collective-permute-start.8 = (f32[64,128]{1,0:T(8,128)}, f32[64,128]{1,0:T(8,128)S(1)}, u32[]{:S(2)}, u32[]{:S(2)}) collective-permute-start(f32[64,128]{1,0:T(8,128)} %get-tuple-element.59), channel_id=1, source_target_pairs={{252,0},{0,4},{4,8},{8,12},{12,16},{16,20},{20,24},{24,28},{28,32}... | collective-permute-start | bytes 98312 | tf_op jit(solution)/shard_map/ppermute | solution.py:12
  132.8 39.2 %collective-permute-start.9 = (f32[64,128]{1,0:T(8,128)}, f32[64,128]{1,0:T(8,128)S(1)}, u32[]{:S(2)}, u32[]{:S(2)}) collective-permute-start(f32[64,128]{1,0:T(8,128)} %get-tuple-element.58), channel_id=1, source_target_pairs={{4,0},{8,4},{12,8},{16,12},{20,16},{24,20},{28,24},{32,28},{36,32}... | collective-permute-start | bytes 98312 | tf_op jit(solution)/shard_map/ppermute | solution.py:12
  139.3 32.7 %collective-permute-start.10 = (f32[64,128]{1,0:T(8,128)}, f32[64,128]{1,0:T(8,128)S(1)}, u32[]{:S(2)}, u32[]{:S(2)}) collective-permute-start(f32[64,128]{1,0:T(8,128)} %get-tuple-element.57), channel_id=1, source_target_pairs={{248,0},{252,4},{0,8},{4,12},{8,16},{12,20},{16,24},{20,28},{24,32... | collective-permute-start | bytes 98312 | tf_op jit(solution)/shard_map/ppermute | solution.py:12
  140.8 36.8 %collective-permute-start.11 = (f32[64,128]{1,0:T(8,128)}, f32[64,128]{1,0:T(8,128)S(1)}, u32[]{:S(2)}, u32[]{:S(2)}) collective-permute-start(f32[64,128]{1,0:T(8,128)} %get-tuple-element.56), channel_id=1, source_target_pairs={{8,0},{12,4},{16,8},{20,12},{24,16},{28,20},{32,24},{36,28},{40,32... | collective-permute-start | bytes 98312 | tf_op jit(solution)/shard_map/ppermute | solution.py:12
  172.1 33.0 %collective-permute-start.43 = (f32[64,128]{0,1:T(8,128)}, f32[64,128]{0,1:T(8,128)}, u32[]{:S(2)}, u32[]{:S(2)}) collective-permute-start(f32[64,128]{0,1:T(8,128)} %get-tuple-element.24), channel_id=1, source_target_pairs={{8,0},{12,4},{16,8},{20,12},{24,16},{28,20},{32,24},{36,28},{40,32... | collective-permute-start | bytes 98312 | tf_op jit(solution)/shard_map/ppermute | solution.py:12
  190.1 38.4 %collective-permute-start.13 = (f32[64,128]{1,0:T(8,128)}, f32[64,128]{1,0:T(8,128)S(1)}, u32[]{:S(2)}, u32[]{:S(2)}) collective-permute-start(f32[64,128]{1,0:T(8,128)} %get-tuple-element.54), channel_id=1, source_target_pairs={{4,0},{8,4},{12,8},{16,12},{20,16},{24,20},{28,24},{32,28},{36,32}... | collective-permute-start | bytes 98312 | tf_op jit(solution)/shard_map/ppermute | solution.py:12
  196.6 33.9 %collective-permute-start.14 = (f32[64,128]{1,0:T(8,128)}, f32[64,128]{1,0:T(8,128)}, u32[]{:S(2)}, u32[]{:S(2)}) collective-permute-start(f32[64,128]{1,0:T(8,128)} %get-tuple-element.53), channel_id=1, source_target_pairs={{248,0},{252,4},{0,8},{4,12},{8,16},{12,20},{16,24},{20,28},{24,32... | collective-permute-start | bytes 98312 | tf_op jit(solution)/shard_map/ppermute | solution.py:12
  198.1 39.6 %collective-permute-start.15 = (f32[64,128]{1,0:T(8,128)}, f32[64,128]{1,0:T(8,128)}, u32[]{:S(2)}, u32[]{:S(2)}) collective-permute-start(f32[64,128]{1,0:T(8,128)} %get-tuple-element.52), channel_id=1, source_target_pairs={{8,0},{12,4},{16,8},{20,12},{24,16},{28,20},{32,24},{36,28},{40,32... | collective-permute-start | bytes 98312 | tf_op jit(solution)/shard_map/ppermute | solution.py:12
  222.8 36.3 %collective-permute-start.45 = (f32[64,128]{0,1:T(8,128)}, f32[64,128]{0,1:T(8,128)S(1)}, u32[]{:S(2)}, u32[]{:S(2)}) collective-permute-start(f32[64,128]{0,1:T(8,128)} %get-tuple-element.22), channel_id=1, source_target_pairs={{4,0},{8,4},{12,8},{16,12},{20,16},{24,20},{28,24},{32,28},{36,32}... | collective-permute-start | bytes 98312 | tf_op jit(solution)/shard_map/ppermute | solution.py:12
  230.5 35.3 %collective-permute-start.47 = (f32[64,128]{0,1:T(8,128)}, f32[64,128]{0,1:T(8,128)}, u32[]{:S(2)}, u32[]{:S(2)}) collective-permute-start(f32[64,128]{0,1:T(8,128)} %get-tuple-element.20), channel_id=1, source_target_pairs={{8,0},{12,4},{16,8},{20,12},{24,16},{28,20},{32,24},{36,28},{40,32... | collective-permute-start | bytes 98312 | tf_op jit(solution)/shard_map/ppermute | solution.py:12
  252.6 34.9 %collective-permute-start.17 = (f32[64,128]{1,0:T(8,128)}, f32[64,128]{1,0:T(8,128)}, u32[]{:S(2)}, u32[]{:S(2)}) collective-permute-start(f32[64,128]{1,0:T(8,128)} %get-tuple-element.50), channel_id=1, source_target_pairs={{4,0},{8,4},{12,8},{16,12},{20,16},{24,20},{28,24},{32,28},{36,32}... | collective-permute-start | bytes 98312 | tf_op jit(solution)/shard_map/ppermute | solution.py:12
  259.7 34.8 %collective-permute-start.19 = (f32[64,128]{1,0:T(8,128)}, f32[64,128]{1,0:T(8,128)}, u32[]{:S(2)}, u32[]{:S(2)}) collective-permute-start(f32[64,128]{1,0:T(8,128)} %get-tuple-element.48), channel_id=1, source_target_pairs={{8,0},{12,4},{16,8},{20,12},{24,16},{28,20},{32,24},{36,28},{40,32... | collective-permute-start | bytes 98312 | tf_op jit(solution)/shard_map/ppermute | solution.py:12
  307.3 34.2 %collective-permute-start.21 = (f32[64,128]{1,0:T(8,128)S(1)}, f32[64,128]{1,0:T(8,128)S(1)}, u32[]{:S(2)}, u32[]{:S(2)}) collective-permute-start(f32[64,128]{1,0:T(8,128)S(1)} %get-tuple-element.46), channel_id=1, source_target_pairs={{4,0},{8,4},{12,8},{16,12},{20,16},{24,20},{28,24},{32,28},{36,32}... | collective-permute-start | bytes 98312 | tf_op jit(solution)/shard_map/ppermute | solution.py:12
  314.4 33.0 %collective-permute-start.23 = (f32[64,128]{1,0:T(8,128)S(1)}, f32[64,128]{1,0:T(8,128)S(1)}, u32[]{:S(2)}, u32[]{:S(2)}) collective-permute-start(f32[64,128]{1,0:T(8,128)S(1)} %get-tuple-element.44), channel_id=1, source_target_pairs={{8,0},{12,4},{16,8},{20,12},{24,16},{28,20},{32,24},{36,28},{40,32... | collective-permute-start | bytes 98312 | tf_op jit(solution)/shard_map/ppermute | solution.py:12
  359.9 34.9 %collective-permute-start.25 = (f32[64,128]{1,0:T(8,128)}, f32[64,128]{1,0:T(8,128)}, u32[]{:S(2)}, u32[]{:S(2)}) collective-permute-start(f32[64,128]{1,0:T(8,128)} %get-tuple-element.42), channel_id=1, source_target_pairs={{4,0},{8,4},{12,8},{16,12},{20,16},{24,20},{28,24},{32,28},{36,32}... | collective-permute-start | bytes 98312 | tf_op jit(solution)/shard_map/ppermute | solution.py:12
  367.1 34.8 %collective-permute-start.27 = (f32[64,128]{1,0:T(8,128)}, f32[64,128]{1,0:T(8,128)}, u32[]{:S(2)}, u32[]{:S(2)}) collective-permute-start(f32[64,128]{1,0:T(8,128)} %get-tuple-element.40), channel_id=1, source_target_pairs={{8,0},{12,4},{16,8},{20,12},{24,16},{28,20},{32,24},{36,28},{40,32... | collective-permute-start | bytes 98312 | tf_op jit(solution)/shard_map/ppermute | solution.py:12
  395.6 33.0 %collective-permute-start.59 = (f32[64,128]{0,1:T(8,128)}, f32[64,128]{0,1:T(8,128)}, u32[]{:S(2)}, u32[]{:S(2)}) collective-permute-start(f32[64,128]{0,1:T(8,128)} %get-tuple-element.8), channel_id=1, source_target_pairs={{8,0},{12,4},{16,8},{20,12},{24,16},{28,20},{32,24},{36,28},{40,32... | collective-permute-start | bytes 98312 | tf_op jit(solution)/shard_map/ppermute | solution.py:12
  415.2 34.4 %collective-permute-start.29 = (f32[64,128]{1,0:T(8,128)}, f32[64,128]{1,0:T(8,128)}, u32[]{:S(2)}, u32[]{:S(2)}) collective-permute-start(f32[64,128]{1,0:T(8,128)} %get-tuple-element.38), channel_id=1, source_target_pairs={{4,0},{8,4},{12,8},{16,12},{20,16},{24,20},{28,24},{32,28},{36,32}... | collective-permute-start | bytes 98312 | tf_op jit(solution)/shard_map/ppermute | solution.py:12
  422.4 34.4 %collective-permute-start.31 = (f32[64,128]{1,0:T(8,128)}, f32[64,128]{1,0:T(8,128)}, u32[]{:S(2)}, u32[]{:S(2)}) collective-permute-start(f32[64,128]{1,0:T(8,128)} %get-tuple-element.36), channel_id=1, source_target_pairs={{8,0},{12,4},{16,8},{20,12},{24,16},{28,20},{32,24},{36,28},{40,32... | collective-permute-start | bytes 98312 | tf_op jit(solution)/shard_map/ppermute | solution.py:12
  (57 other events, 1124.3 us)
Sparse Core Ops, SparseCore 0:
  473.9 181.1 all-reduce.1
where the time goes:
time: 673 us; the launch traced here: 664 us
  waiting for transfers between devices  187 us (28%)
  starting transfers between devices  164 us (24%)
  matrix products  131 us (19%)
  local copies, waits for them, and re-layouts  127 us (19%)
  blocking collectives  26.5 us (4%)
  between operations  15.7 us (2%)
  other arithmetic  13 us (2%)
    psum x1, waiting for transfers between devices, local(): summed = lax.psum(local_grads, 'dom')  173 us
    ppermute x64, starting transfers between devices, from_behind(): return lax.ppermute(block, axis, route)  163 us
    dot_general x16, matrix products, apply_operator(): jnp.einsum('ctj,tjk->ctk', picked, tile_values, precision=lax.Precision.H...  107 us
    unnamed x82, local copies, waits for them, and re-layouts  37.6 us
    gather x16, local copies, waits for them, and re-layouts, apply_operator(): picked = jnp.take(blocks, tile_cols.reshape(-1), axis=1)  31.3 us
    gather x24, local copies, waits for them, and re-layouts, apply_operator(): outgoing = jnp.take(field_in, send_list[0], axis=1)  18 us
    concatenate x16, local copies, waits for them, and re-layouts, apply_operator(): extended = jnp.concatenate([field_in] + received, axis=1)  14.5 us
    ppermute x64, waiting for transfers between devices, from_behind(): return lax.ppermute(block, axis, route)  14 us
  transfers between devices with their start and end apart: 65, of which 4 were waited for; matrix products, arithmetic and copies ran while one was open for 36% of the time, Pallas kernels for 0%

commit v1 on v0

--- a/solution.py
+++ b/solution.py
@@ -44,7 +44,9 @@
 
     feat_all, cot_all = (
         lax.all_gather(features, "chan", axis=0, tiled=True),
-        lax.all_gather(cotangent, "chan", axis=0, tiled=True),
+        jnp.concatenate(
+            lax.all_to_all(jnp.stack([cotangent] * lax.axis_size("chan")), "chan", 0, 0), axis=0
+        ),
     )
     feat_wide = feat_all.astype(jnp.float32)
 

time: 673 us -> 611 us (0.908)
  local copies, waits for them, and re-layouts: 127 us -> 74.4 us
  blocking collectives: 26.5 us -> 13.4 us
  starting transfers between devices: 164 us -> 176 us
    unnamed x82 -> x80, local copies, waits for them, and re-layouts: 37.6 us -> 9.93 us
    all_gather x1 -> x0, blocking collectives: 13.7 us -> none  [local(): lax.all_gather(cotangent, 'chan', axis=0, tiled=True)]
    concatenate x16, local copies, waits for them, and re-layouts: 14.5 us -> 1.94 us  [apply_operator(): extended = jnp.concatenate([field_in] + received, axis=1)]
    psum x1, waiting for transfers between devices: 173 us -> 163 us  [local(): summed = lax.psum(local_grads, 'dom')]
    ppermute x64, waiting for transfers between devices: 14 us -> 22.3 us  [from_behind(): return lax.ppermute(block, axis, route)]
    squeeze x16, local copies, waits for them, and re-layouts: 8.17 us -> 0.91 us  [exchange_rows(): outgoing[:, slot_index]]
  transfers between devices with their start and end apart: 65 -> 66, of which waited for: 4 -> 18; matrix products, arithmetic and copies ran while one was open for 36% -> 26% of each run, Pallas kernels for 0% -> 0%
where the time goes in v1:
time: 611 us; the launch traced here: 602 us
  waiting for transfers between devices  185 us (30%)
  starting transfers between devices  176 us (29%)
  matrix products  126 us (21%)
  local copies, waits for them, and re-layouts  74.4 us (12%)
  between operations  15.8 us (3%)
  blocking collectives  13.4 us (2%)
  other arithmetic  11.6 us (2%)
    ppermute x64, starting transfers between devices, from_behind(): return lax.ppermute(block, axis, route)  170 us
    psum x1, waiting for transfers between devices, local(): summed = lax.psum(local_grads, 'dom')  163 us
    dot_general x16, matrix products, apply_operator(): jnp.einsum('ctj,tjk->ctk', picked, tile_values, precision=lax.Precision.H...  104 us
    gather x16, local copies, waits for them, and re-layouts, apply_operator(): picked = jnp.take(blocks, tile_cols.reshape(-1), axis=1)  27.1 us
    ppermute x64, waiting for transfers between devices, from_behind(): return lax.ppermute(block, axis, route)  22.3 us
    gather x24, local copies, waits for them, and re-layouts, apply_operator(): outgoing = jnp.take(field_in, send_list[0], axis=1)  20.6 us
    all_gather x1, blocking collectives, local(): lax.all_gather(features, 'chan', axis=0, tiled=True)  13.4 us
  transfers between devices with their start and end apart: 66, of which 18 were waited for; matrix products, arithmetic and copies ran while one was open for 26% of the time, Pallas kernels for 0%

profile of v1, /device:TPU:2, one launch (start us, length us, event | category | flops | bytes accessed | tf_op | source)
XLA Modules:
  0.0 602.3 jit_solution(6355846648055474403)
XLA Ops:
  9.0 5.7 all-to-all-start
  18.6 6.4 %collective-permute-start.33 = (f32[64,128]{0,1:T(8,128)S(1)}, f32[64,128]{0,1:T(8,128)S(1)}, u32[]{:S(2)}, u32[]{:S(2)}) collective-permute-start(f32[64,128]{0,1:T(8,128)S(1)} %get-tuple-element.34), channel_id=1, source_target_pairs={{4,0},{8,4},{12,8},{16,12},{20,16},{24,20},{28,24},{32,28},{36,32}... | collective-permute-start | bytes 98312 | tf_op jit(solution)/shard_map/ppermute | solution.py:12
  30.4 13.4 %all_gather.3 = bf16[256,1024]{1,0:T(8,128)(2,1)S(1)} all-gather(bf16[64,1024]{1,0:T(8,128)(2,1)S(1)} %copy-done.13), channel_id=1, replica_groups=mesh['dom'=64,'chan'=4] {'chan'}, dimensions={0}, use_global_device_ids=true | all-gather | bytes 655360 | tf_op jit(solution)/shard_map/all_gather | solution.py:46
  45.8 6.4 %bitcast_reduce_fusion.7 = f32[64,8,128]{2,0,1:T(8,128)} fusion(f32[64,128,128]{2,1,0:T(8,128)} %param.13, f32[64,64,128]{2,1,0:T(8,128)S(1)} %gather_fusion.17, pred[64]{0:T(512)(128)(4,1)S(1)} %compare_and_fusion), kind=kOutput, calls=%fused_computation.39 | convolution fusion | flops 806289408 | bytes 6553664 | tf_op jit(solution)/shard_map/ctj,tjk->ctk/dot_general | solution.py:32
  71.0 6.7 %bitcast_reduce_fusion.6 = f32[64,8,128]{2,0,1:T(8,128)S(1)} fusion(f32[64,128,128]{2,1,0:T(8,128)} %param.13, f32[64,64,128]{2,1,0:T(8,128)} %gather_fusion.19, pred[64]{0:T(512)(128)(4,1)S(1)} %compare_and_fusion), kind=kOutput, calls=%fused_computation.38 | convolution fusion | flops 806289408 | bytes 6553664 | tf_op jit(solution)/shard_map/ctj,tjk->ctk/dot_general | solution.py:32
  97.3 6.7 %bitcast_reduce_fusion.5 = f32[64,8,128]{2,0,1:T(8,128)S(1)} fusion(f32[64,128,128]{2,1,0:T(8,128)} %param.13, f32[64,64,128]{2,1,0:T(8,128)} %gather_fusion.21, pred[64]{0:T(512)(128)(4,1)S(1)} %compare_and_fusion), kind=kOutput, calls=%fused_computation.37 | convolution fusion | flops 806289408 | bytes 6553664 | tf_op jit(solution)/shard_map/ctj,tjk->ctk/dot_general | solution.py:32
  113.8 5.6 collective-permute-start.47
  123.7 6.7 %bitcast_reduce_fusion.4 = f32[64,8,128]{2,0,1:T(8,128)S(1)} fusion(f32[64,128,128]{2,1,0:T(8,128)} %param.13, f32[64,64,128]{2,1,0:T(8,128)} %gather_fusion.23, pred[64]{0:T(512)(128)(4,1)S(1)} %compare_and_fusion), kind=kOutput, calls=%fused_computation.36 | convolution fusion | flops 806289408 | bytes 6553664 | tf_op jit(solution)/shard_map/ctj,tjk->ctk/dot_general | solution.py:32
  139.1 5.8 collective-permute-start.51
  151.4 6.7 %bitcast_reduce_fusion.3 = f32[64,8,128]{2,0,1:T(8,128)S(1)} fusion(f32[64,128,128]{2,1,0:T(8,128)} %param.13, f32[64,64,128]{2,1,0:T(8,128)} %gather_fusion.25, pred[64]{0:T(512)(128)(4,1)S(1)} %compare_and_fusion), kind=kOutput, calls=%fused_computation.35 | convolution fusion | flops 806289408 | bytes 6553664 | tf_op jit(solution)/shard_map/ctj,tjk->ctk/dot_general | solution.py:32
  179.0 6.7 %bitcast_reduce_fusion.2 = f32[64,8,128]{2,0,1:T(8,128)S(1)} fusion(f32[64,128,128]{2,1,0:T(8,128)} %param.13, f32[64,64,128]{2,1,0:T(8,128)} %gather_fusion.27, pred[64]{0:T(512)(128)(4,1)S(1)} %compare_and_fusion), kind=kOutput, calls=%fused_computation.34 | convolution fusion | flops 806289408 | bytes 6553664 | tf_op jit(solution)/shard_map/ctj,tjk->ctk/dot_general | solution.py:32
  204.3 6.7 %bitcast_reduce_fusion.1 = f32[64,8,128]{2,0,1:T(8,128)S(1)} fusion(f32[64,128,128]{2,1,0:T(8,128)} %param.13, f32[64,64,128]{2,1,0:T(8,128)} %gather_fusion.29, pred[64]{0:T(512)(128)(4,1)S(1)} %compare_and_fusion), kind=kOutput, calls=%fused_computation.33 | convolution fusion | flops 806289408 | bytes 6553664 | tf_op jit(solution)/shard_map/ctj,tjk->ctk/dot_general | solution.py:32
  236.7 5.6 collective-permute-start.3
  246.0 6.7 %bitcast_reduce_fusion.15 = f32[64,8,128]{2,0,1:T(8,128)S(1)} fusion(f32[64,128,128]{2,1,0:T(8,128)} %param.13, f32[64,64,128]{2,1,0:T(8,128)} %gather_fusion.1, pred[64]{0:T(512)(128)(4,1)S(1)} %compare_and_fusion), kind=kOutput, calls=%fused_computation.47 | convolution fusion | flops 806289408 | bytes 6553664 | tf_op jit(solution)/shard_map/ctj,tjk->ctk/dot_general | solution.py:32
  270.1 6.7 %bitcast_reduce_fusion.14 = f32[64,8,128]{2,0,1:T(8,128)S(1)} fusion(f32[64,128,128]{2,1,0:T(8,128)} %param.13, f32[64,64,128]{2,1,0:T(8,128)} %gather_fusion.3, pred[64]{0:T(512)(128)(4,1)S(1)} %compare_and_fusion), kind=kOutput, calls=%fused_computation.46 | convolution fusion | flops 806289408 | bytes 6553664 | tf_op jit(solution)/shard_map/ctj,tjk->ctk/dot_general | solution.py:32
  298.3 6.7 %bitcast_reduce_fusion.13 = f32[64,8,128]{2,0,1:T(8,128)S(1)} fusion(f32[64,128,128]{2,1,0:T(8,128)} %param.13, f32[64,64,128]{2,1,0:T(8,128)} %gather_fusion.5, pred[64]{0:T(512)(128)(4,1)S(1)} %compare_and_fusion), kind=kOutput, calls=%fused_computation.45 | convolution fusion | flops 806289408 | bytes 6553664 | tf_op jit(solution)/shard_map/ctj,tjk->ctk/dot_general | solution.py:32
  307.5 6.7 %bitcast_reduce_fusion = f32[64,8,128]{2,0,1:T(8,128)S(1)} fusion(f32[64,128,128]{2,1,0:T(8,128)} %param.13, f32[64,64,128]{2,1,0:T(8,128)} %gather_fusion.31, pred[64]{0:T(512)(128)(4,1)S(1)} %compare_and_fusion), kind=kOutput, calls=%fused_computation.32 | convolution fusion | flops 806289408 | bytes 6553664 | tf_op jit(solution)/shard_map/ctj,tjk->ctk/dot_general | solution.py:32
  319.3 5.7 collective-permute-start.15
  328.7 6.7 %bitcast_reduce_fusion.12 = f32[64,8,128]{2,0,1:T(8,128)S(1)} fusion(f32[64,128,128]{2,1,0:T(8,128)} %param.13, f32[64,64,128]{2,1,0:T(8,128)} %gather_fusion.7, pred[64]{0:T(512)(128)(4,1)S(1)} %compare_and_fusion), kind=kOutput, calls=%fused_computation.44 | convolution fusion | flops 806289408 | bytes 6553664 | tf_op jit(solution)/shard_map/ctj,tjk->ctk/dot_general | solution.py:32
  355.5 6.7 %bitcast_reduce_fusion.11 = f32[64,8,128]{2,0,1:T(8,128)S(1)} fusion(f32[64,128,128]{2,1,0:T(8,128)} %param.13, f32[64,64,128]{2,1,0:T(8,128)} %gather_fusion.9, pred[64]{0:T(512)(128)(4,1)S(1)} %compare_and_fusion), kind=kOutput, calls=%fused_computation.43 | convolution fusion | flops 806289408 | bytes 6553664 | tf_op jit(solution)/shard_map/ctj,tjk->ctk/dot_general | solution.py:32
  380.9 5.7 bitcast_reduce_fusion.10
  403.7 5.7 bitcast_reduce_fusion.9
  411.9 162.8 %all-reduce.2.cloned.1.call-done = f32[9,256,64]{1,2,0:T(8,128)} async-done(((f32[9,256,64]{1,2,0:T(8,128)}), f32[9,256,64]{1,2,0:T(8,128)}) %all-reduce.2.cloned.1.call-update) | async-done | bytes 589840 | tf_op jit(solution)/shard_map/psum | solution.py:77
  587.9 5.7 bitcast_reduce_fusion.8
  (368 shorter events, 271.7 us)
Async XLA Ops:
  9.0 217.8 %all-to-all-start = ((bf16[4,64,1024]{2,1,0:T(8,128)(2,1)}), bf16[4,64,1024]{2,1,0:T(8,128)(2,1)S(1)}, u32[]{:S(2)}, u32[]{:S(2)}) async-start(bf16[4,64,1024]{2,1,0:T(8,128)(2,1)} %stack.37), calls=%async_computation | async-start | bytes 1048576 | tf_op jit(solution)/shard_map/all_to_all | solution.py:48
  14.7 560.0 %all-reduce.2.cloned.1.call-start = ((), (), s32[]{:S(2)}) async-start(), calls=%async_computation.1 | async-start | bytes 1179648 | tf_op jit(solution)/shard_map/psum | solution.py:77
  18.5 26.3 %collective-permute-start.32 = (f32[64,128]{0,1:T(8,128)S(1)}, f32[64,128]{0,1:T(8,128)S(1)}, u32[]{:S(2)}, u32[]{:S(2)}) collective-permute-start(f32[64,128]{0,1:T(8,128)S(1)} %get-tuple-element.35), channel_id=1, source_target_pairs={{252,0},{0,4},{4,8},{8,12},{12,16},{16,20},{20,24},{24,28},{28,32}... | collective-permute-start | bytes 98312 | tf_op jit(solution)/shard_map/ppermute | solution.py:12
  18.6 26.2 %collective-permute-start.33 = (f32[64,128]{0,1:T(8,128)S(1)}, f32[64,128]{0,1:T(8,128)S(1)}, u32[]{:S(2)}, u32[]{:S(2)}) collective-permute-start(f32[64,128]{0,1:T(8,128)S(1)} %get-tuple-element.34), channel_id=1, source_target_pairs={{4,0},{8,4},{12,8},{16,12},{20,16},{24,20},{28,24},{32,28},{36,32}... | collective-permute-start | bytes 98312 | tf_op jit(solution)/shard_map/ppermute | solution.py:12
  25.0 19.8 %collective-permute-start.34 = (f32[64,128]{0,1:T(8,128)S(1)}, f32[64,128]{0,1:T(8,128)S(1)}, u32[]{:S(2)}, u32[]{:S(2)}) collective-permute-start(f32[64,128]{0,1:T(8,128)S(1)} %get-tuple-element.33), channel_id=1, source_target_pairs={{248,0},{252,4},{0,8},{4,12},{8,16},{12,20},{16,24},{20,28},{24,32... | collective-permute-start | bytes 98312 | tf_op jit(solution)/shard_map/ppermute | solution.py:12
  25.0 19.8 %collective-permute-start.35 = (f32[64,128]{0,1:T(8,128)S(1)}, f32[64,128]{0,1:T(8,128)S(1)}, u32[]{:S(2)}, u32[]{:S(2)}) collective-permute-start(f32[64,128]{0,1:T(8,128)S(1)} %get-tuple-element.32), channel_id=1, source_target_pairs={{8,0},{12,4},{16,8},{20,12},{24,16},{28,20},{32,24},{36,28},{40,32... | collective-permute-start | bytes 98312 | tf_op jit(solution)/shard_map/ppermute | solution.py:12
  81.1 11.9 %collective-permute-start.40 = (f32[64,128]{0,1:T(8,128)S(1)}, f32[64,128]{0,1:T(8,128)S(1)}, u32[]{:S(2)}, u32[]{:S(2)}) collective-permute-start(f32[64,128]{0,1:T(8,128)S(1)} %get-tuple-element.27), channel_id=1, source_target_pairs={{252,0},{0,4},{4,8},{8,12},{12,16},{16,20},{20,24},{24,28},{28,32}... | collective-permute-start | bytes 98312 | tf_op jit(solution)/shard_map/ppermute | solution.py:12
  107.5 11.9 %collective-permute-start.44 = (f32[64,128]{0,1:T(8,128)S(1)}, f32[64,128]{0,1:T(8,128)S(1)}, u32[]{:S(2)}, u32[]{:S(2)}) collective-permute-start(f32[64,128]{0,1:T(8,128)S(1)} %get-tuple-element.23), channel_id=1, source_target_pairs={{252,0},{0,4},{4,8},{8,12},{12,16},{16,20},{20,24},{24,28},{28,32}... | collective-permute-start | bytes 98312 | tf_op jit(solution)/shard_map/ppermute | solution.py:12
  132.7 12.2 %collective-permute-start.48 = (f32[64,128]{0,1:T(8,128)S(1)}, f32[64,128]{0,1:T(8,128)S(1)}, u32[]{:S(2)}, u32[]{:S(2)}) collective-permute-start(f32[64,128]{0,1:T(8,128)S(1)} %get-tuple-element.19), channel_id=1, source_target_pairs={{252,0},{0,4},{4,8},{8,12},{12,16},{16,20},{20,24},{24,28},{28,32}... | collective-permute-start | bytes 98312 | tf_op jit(solution)/shard_map/ppermute | solution.py:12
  134.1 11.5 %collective-permute-start.49 = (f32[64,128]{0,1:T(8,128)S(1)}, f32[64,128]{0,1:T(8,128)S(1)}, u32[]{:S(2)}, u32[]{:S(2)}) collective-permute-start(f32[64,128]{0,1:T(8,128)S(1)} %get-tuple-element.18), channel_id=1, source_target_pairs={{4,0},{8,4},{12,8},{16,12},{20,16},{24,20},{28,24},{32,28},{36,32}... | collective-permute-start | bytes 98312 | tf_op jit(solution)/shard_map/ppermute | solution.py:12
  160.4 11.9 %collective-permute-start.52 = (f32[64,128]{0,1:T(8,128)S(1)}, f32[64,128]{0,1:T(8,128)S(1)}, u32[]{:S(2)}, u32[]{:S(2)}) collective-permute-start(f32[64,128]{0,1:T(8,128)S(1)} %get-tuple-element.15), channel_id=1, source_target_pairs={{252,0},{0,4},{4,8},{8,12},{12,16},{16,20},{20,24},{24,28},{28,32}... | collective-permute-start | bytes 98312 | tf_op jit(solution)/shard_map/ppermute | solution.py:12
  161.7 11.2 %collective-permute-start.53 = (f32[64,128]{0,1:T(8,128)S(1)}, f32[64,128]{0,1:T(8,128)S(1)}, u32[]{:S(2)}, u32[]{:S(2)}) collective-permute-start(f32[64,128]{0,1:T(8,128)S(1)} %get-tuple-element.14), channel_id=1, source_target_pairs={{4,0},{8,4},{12,8},{16,12},{20,16},{24,20},{28,24},{32,28},{36,32}... | collective-permute-start | bytes 98312 | tf_op jit(solution)/shard_map/ppermute | solution.py:12
  188.1 11.9 %collective-permute-start.56 = (f32[64,128]{0,1:T(8,128)S(1)}, f32[64,128]{0,1:T(8,128)S(1)}, u32[]{:S(2)}, u32[]{:S(2)}) collective-permute-start(f32[64,128]{0,1:T(8,128)S(1)} %get-tuple-element.11), channel_id=1, source_target_pairs={{252,0},{0,4},{4,8},{8,12},{12,16},{16,20},{20,24},{24,28},{28,32}... | collective-permute-start | bytes 98312 | tf_op jit(solution)/shard_map/ppermute | solution.py:12
  215.1 11.6 %collective-permute-start.60 = (f32[64,128]{0,1:T(8,128)S(1)}, f32[64,128]{0,1:T(8,128)S(1)}, u32[]{:S(2)}, u32[]{:S(2)}) collective-permute-start(f32[64,128]{0,1:T(8,128)S(1)} %get-tuple-element.7), channel_id=1, source_target_pairs={{252,0},{0,4},{4,8},{8,12},{12,16},{16,20},{20,24},{24,28},{28,32}... | collective-permute-start | bytes 98312 | tf_op jit(solution)/shard_map/ppermute | solution.py:12
  216.3 13.8 %collective-permute-start.61 = (f32[64,128]{0,1:T(8,128)}, f32[64,128]{0,1:T(8,128)}, u32[]{:S(2)}, u32[]{:S(2)}) collective-permute-start(f32[64,128]{0,1:T(8,128)} %get-tuple-element.6), channel_id=1, source_target_pairs={{4,0},{8,4},{12,8},{16,12},{20,16},{24,20},{28,24},{32,28},{36,32}... | collective-permute-start | bytes 98312 | tf_op jit(solution)/shard_map/ppermute | solution.py:12
  221.3 33.8 %collective-permute-start.62 = (f32[64,128]{0,1:T(8,128)}, f32[64,128]{0,1:T(8,128)S(1)}, u32[]{:S(2)}, u32[]{:S(2)}) collective-permute-start(f32[64,128]{0,1:T(8,128)} %get-tuple-element.5), channel_id=1, source_target_pairs={{248,0},{252,4},{0,8},{4,12},{8,16},{12,20},{16,24},{20,28},{24,32... | collective-permute-start | bytes 98312 | tf_op jit(solution)/shard_map/ppermute | solution.py:12
  221.3 60.2 %collective-permute-start.63 = (f32[64,128]{0,1:T(8,128)}, f32[64,128]{0,1:T(8,128)S(1)}, u32[]{:S(2)}, u32[]{:S(2)}) collective-permute-start(f32[64,128]{0,1:T(8,128)} %get-tuple-element.4), channel_id=1, source_target_pairs={{8,0},{12,4},{16,8},{20,12},{24,16},{28,20},{32,24},{36,28},{40,32... | collective-permute-start | bytes 98312 | tf_op jit(solution)/shard_map/ppermute | solution.py:12
  255.1 11.3 %collective-permute-start.4 = (f32[64,128]{1,0:T(8,128)S(1)}, f32[64,128]{1,0:T(8,128)S(1)}, u32[]{:S(2)}, u32[]{:S(2)}) collective-permute-start(f32[64,128]{1,0:T(8,128)S(1)} %get-tuple-element.63), channel_id=1, source_target_pairs={{252,0},{0,4},{4,8},{8,12},{12,16},{16,20},{20,24},{24,28},{28,32}... | collective-permute-start | bytes 98312 | tf_op jit(solution)/shard_map/ppermute | solution.py:12
  281.5 13.0 %collective-permute-start.8 = (f32[64,128]{1,0:T(8,128)S(1)}, f32[64,128]{1,0:T(8,128)S(1)}, u32[]{:S(2)}, u32[]{:S(2)}) collective-permute-start(f32[64,128]{1,0:T(8,128)S(1)} %get-tuple-element.59), channel_id=1, source_target_pairs={{252,0},{0,4},{4,8},{8,12},{12,16},{16,20},{20,24},{24,28},{28,32}... | collective-permute-start | bytes 98312 | tf_op jit(solution)/shard_map/ppermute | solution.py:12
  307.4 17.6 %collective-permute-start.12 = (f32[64,128]{1,0:T(8,128)S(1)}, f32[64,128]{1,0:T(8,128)S(1)}, u32[]{:S(2)}, u32[]{:S(2)}) collective-permute-start(f32[64,128]{1,0:T(8,128)S(1)} %get-tuple-element.55), channel_id=1, source_target_pairs={{252,0},{0,4},{4,8},{8,12},{12,16},{16,20},{20,24},{24,28},{28,32}... | collective-permute-start | bytes 98312 | tf_op jit(solution)/shard_map/ppermute | solution.py:12
  338.8 11.2 %collective-permute-start.17 = (f32[64,128]{1,0:T(8,128)S(1)}, f32[64,128]{1,0:T(8,128)S(1)}, u32[]{:S(2)}, u32[]{:S(2)}) collective-permute-start(f32[64,128]{1,0:T(8,128)S(1)} %get-tuple-element.50), channel_id=1, source_target_pairs={{4,0},{8,4},{12,8},{16,12},{20,16},{24,20},{28,24},{32,28},{36,32}... | collective-permute-start | bytes 98312 | tf_op jit(solution)/shard_map/ppermute | solution.py:12
  366.8 11.4 %collective-permute-start.20 = (f32[64,128]{1,0:T(8,128)S(1)}, f32[64,128]{1,0:T(8,128)S(1)}, u32[]{:S(2)}, u32[]{:S(2)}) collective-permute-start(f32[64,128]{1,0:T(8,128)S(1)} %get-tuple-element.47), channel_id=1, source_target_pairs={{252,0},{0,4},{4,8},{8,12},{12,16},{16,20},{20,24},{24,28},{28,32}... | collective-permute-start | bytes 98312 | tf_op jit(solution)/shard_map/ppermute | solution.py:12
  389.0 12.0 %collective-permute-start.24 = (f32[64,128]{1,0:T(8,128)S(1)}, f32[64,128]{1,0:T(8,128)S(1)}, u32[]{:S(2)}, u32[]{:S(2)}) collective-permute-start(f32[64,128]{1,0:T(8,128)S(1)} %get-tuple-element.43), channel_id=1, source_target_pairs={{252,0},{0,4},{4,8},{8,12},{12,16},{16,20},{20,24},{24,28},{28,32}... | collective-permute-start | bytes 98312 | tf_op jit(solution)/shard_map/ppermute | solution.py:12
  411.8 173.4 %collective-permute-start.28 = (f32[64,128]{1,0:T(8,128)S(1)}, f32[64,128]{1,0:T(8,128)S(1)}, u32[]{:S(2)}, u32[]{:S(2)}) collective-permute-start(f32[64,128]{1,0:T(8,128)S(1)} %get-tuple-element.39), channel_id=1, source_target_pairs={{252,0},{0,4},{4,8},{8,12},{12,16},{16,20},{20,24},{24,28},{28,32}... | collective-permute-start | bytes 98312 | tf_op jit(solution)/shard_map/ppermute | solution.py:12
  (57 other events, 501.4 us)
Sparse Core Ops, SparseCore 0:
  390.5 184.1 all-reduce.1
